TPU v7x, 32 devices: a whole 2x2x4 slice. The times are simulated.
32 devices in a mesh: dp: 4 (over y, x), vocab: 8 (over z, core).
Axes of the slice: x: 2, y: 2, z: 4, core: 2. Of those that a mesh axis runs over, the one named last changes fastest.
Arguments:
- hidden: bfloat16 [192, 4096], P(('dp', 'vocab')), may hold values from -240 to 240
- head_weight: bfloat16 [4096, 163840], P(None, ('dp', 'vocab')), may hold values from -0.40625 to 0.40625
- targets: int32 [192], P(('dp', 'vocab')), may hold values from 0 to 163839, as said below
- image_mask: int32 [192], P(('dp', 'vocab')), may hold values from 0 to 1
- lengths: int32 [4], replicated, may hold values from 12 to 48, as said below
- ref_logps: float32 [4], replicated, may hold values from -18 to -13
- pairing: int32 [4], replicated, may hold values from 0 to 3, each once
Outputs:
- grad_hidden: bfloat16 [192, 4096], P(('dp', 'vocab'))
- grad_head: bfloat16 [4096, 163840], P(None, ('dp', 'vocab'))
- mean_loss: float32 [], replicated
Inputs may be any that keep to these rules, and one draw needn't show every extreme that they name: `targets`: each token's target lies in its modality's columns: at least 131072 where image_mask is 1, below it where image_mask is 0. `lengths`: some window is full.
All inputs are finite; a program needn't handle non-finite values.
Results may differ from a plain program's by a relative error of at most 0.0067.
Values may be sent and summed in bfloat16 or wider, within the bound.
A program may use at most 192 MiB of HBM per device.

v0:
```python
import functools

import jax
import jax.numpy as jnp
from jax import lax
from jax.experimental import pallas as pl
from jax.experimental.pallas import tpu as pltpu
from jax.sharding import PartitionSpec as P

V = 163840
CODES = 32768
WIN = 48

NEG = -1e30
BETA = 1.0
LOSS_SCALE = 4096.0

AG_CHUNKS = 4
AHEAD = 2
RS_CHUNKS = 4
LANES = 128
MESH = pl.DeviceIdType.MESH
F32 = jnp.float32
BF16 = jnp.bfloat16


def block_of(size):
    for block in (512, 256, 128):
        if size % block == 0:
            return block


def flip(x, mask):
    bit = 1
    while bit <= mask:
        if mask & bit:
            x = x + bit - 2 * bit * lax.rem(x // bit, 2)
        bit *= 2
    return x


def main_kernel(cfg, targets, lengths, ref_logps, pairing, hidden, w_hbm, gh, g_hbm, h_hbm, loss,
                w, hid, h, logits, g, r1, tgt, norm_b, weight_b, packed, spread, sb1, rb1, sb2, rb2,
                s1, b1, acc, s2, b2, s3, b3,
                w_sem, a1s, a1r, a2s, a2r, a3s, a3r, t1s, t1r, t2s, t2r,
                c1s, c1r, c2s, c2r, c3s, c3r, out_sem):
    n_dp, n_v = cfg["n_dp"], cfg["n_v"]
    bits = n_dp.bit_length() - 1
    tokens, columns = g.shape
    half = w.shape[0] // 2
    wide = half + LANES
    rows = tokens // (n_dp * n_v)
    me = lax.axis_index("dp")
    mv = lax.axis_index("vocab")
    core = lax.rem(mv, 2)
    mate = mv + 1 - 2 * core
    peers = [lax.rem(mv + o, n_v) for o in range(1, n_v)]
    groups = [lax.rem(me + o, n_dp) for o in range(1, n_dp)]

    step = half // AG_CHUNKS
    spans = [(j * step, step) for j in range(AG_CHUNKS)]

    loads = []
    for j, (at, size) in enumerate(spans):
        for side in range(2):
            span = pl.ds(side * half + at, size)
            loads.append(pltpu.make_async_copy(w_hbm.at[span, :], w.at[span, :], w_sem.at[2 * j + side]))
            loads[-1].start()

    spot = lax.broadcasted_iota(jnp.int32, (8, LANES), 0)
    digit = lax.broadcasted_iota(jnp.int32, (8, LANES), 1)
    tail = jnp.zeros((8, LANES), F32)
    for r in range(rows):
        number = targets[r]
        high, middle, low = number // 65536, lax.rem(number // 256, 256), lax.rem(number, 256)
        value = jnp.where(digit == 0, high, jnp.where(digit == 1, middle, low)).astype(F32)
        tail = jnp.where(spot == r, value, tail)
    hid[...] = jnp.zeros_like(hid)
    for side in range(2):
        hid[0:rows, side * wide:side * wide + half] = hidden[:, side * half:side * half + half]
        hid[:, side * wide + half:side * wide + wide] = tail.astype(BF16)

    barrier = pltpu.get_barrier_semaphore()
    for v in peers:
        pl.semaphore_signal(barrier, inc=1, device_id=(me, v), device_id_type=MESH)
    for d in groups:
        pl.semaphore_signal(barrier, inc=1, device_id=(d, mv), device_id_type=MESH)
    pl.semaphore_wait(barrier, n_v - 1 + n_dp - 1)

    sent = []

    def send(src, dst, s_sem, r_sem, device):
        copy = pltpu.make_async_remote_copy(
            src_ref=src, dst_ref=dst, send_sem=s_sem, recv_sem=r_sem, device_id=device, device_id_type=MESH)
        copy.start()
        sent.append(copy)
        return copy

    def pick(a, b):
        return a + core * (b - a)

    def route(s):
        partner = pick(flip(me, 1 << s), flip(me, 1 << (bits - 1 - s)))
        held = []
        for k in range(1 << s):
            held.append(pick(flip(me, k), flip(me, k << (bits - s))))
        far = []
        for k in range(1 << s):
            far.append(pick(flip(me, k | (1 << s)), flip(me, (k << (bits - s)) | (1 << (bits - 1 - s)))))
        return partner, held, far

    routes = [route(s) for s in range(bits)]

    def window(index):
        return pl.ds(pl.multiple_of(index * WIN, 16), WIN)

    padded = n_v * 8
    r_id = lax.broadcasted_iota(jnp.int32, (WIN, padded), 0)
    s_id = lax.broadcasted_iota(jnp.int32, (WIN, padded), 1)
    perm = jnp.zeros((WIN, padded), F32)
    for v in range(n_v):
        perm = jnp.where((s_id - 8 * v == r_id - rows * v) & (s_id >= 8 * v) & (s_id < 8 * v + rows), 1.0, perm)
    perm = perm.astype(BF16)

    def wire(j):
        at, size = spans[j]
        return at, size + (LANES if j == AG_CHUNKS - 1 else 0)

    first = {}

    def spread_rows(j):
        at, size = wire(j)
        copies = []
        for o, v in enumerate(peers):
            col = pl.multiple_of(lax.rem(v, 2) * wide + at, LANES)
            copies.append(send(hid.at[:, pl.ds(col, size)], r1.at[mv, :, pl.ds(at, size)],
                               a1s.at[j * n_v + o], a1r.at[j * n_v + o], (me, v)))
        first[j] = copies

    for j in range(min(AHEAD, AG_CHUNKS)):
        spread_rows(j)

    waiting = {}

    def mine(j):
        at, size = wire(j)
        return pl.ds(pl.multiple_of(core * wide + at, LANES), size)

    def gather_stage(j, k):
        at, size = wire(j)
        if k == 0:
            r1[mv, :, at:at + size] = hid[:, mine(j)]
            for copy in first[j]:
                copy.wait_recv()
            if j + AHEAD < AG_CHUNKS:
                spread_rows(j + AHEAD)
            block = r1[:, :, at:at + size].astype(F32).reshape(padded, size).astype(BF16)
            h[window(me), mine(j)] = jnp.dot(perm, block, preferred_element_type=F32).astype(BF16)
        else:
            for copy in waiting[j]:
                copy.wait_recv()
        if k < bits:
            partner, held, _ = routes[k]
            copies = []
            for i, d in enumerate(held):
                ref = h.at[window(d), mine(j)]
                sem = j * (n_dp - 1) + (1 << k) - 1 + i
                copies.append(send(ref, ref, a2s.at[sem], a2r.at[sem], (partner, mv)))
            waiting[j] = copies
        elif k == bits:
            ref = h.at[:, mine(j)]
            waiting[j] = [send(ref, ref, a3s.at[j], a3r.at[j], (me, mate))]
        else:
            multiply(j)

    block = block_of(columns)

    def multiply(j):
        at, size = spans[j]
        loads[2 * j].wait()
        loads[2 * j + 1].wait()

        def body(n, carry):
            cols = pl.ds(pl.multiple_of(n * block, block), block)
            part = jnp.dot(h[:, at:at + size], w[at:at + size, cols], preferred_element_type=F32)
            part += jnp.dot(h[:, wide + at:wide + at + size], w[half + at:half + at + size, cols],
                            preferred_element_type=F32)
            logits[:, cols] = part if j == 0 else logits[:, cols] + part
            return carry

        lax.fori_loop(0, columns // block, body, 0)

    for t in range(AG_CHUNKS + bits + 1):
        for k in range(bits + 2):
            if 0 <= t - k < AG_CHUNKS:
                gather_stage(t - k, k)

    h_out = [
        pltpu.make_async_copy(h.at[:, pl.ds(side * wide, half)], h_hbm.at[:, pl.ds(side * half, half)],
                              out_sem.at[side])
        for side in range(2)
    ]
    for copy in h_out:
        copy.start()

    digits = h[:, half:half + LANES].astype(F32)
    target = digits[:, 0:1] * 65536.0 + digits[:, 1:2] * 256.0 + digits[:, 2:3]
    tgt[...] = jnp.broadcast_to(target, (tokens, LANES))
    first_column = (me * n_v + mv) * columns
    lane = lax.broadcasted_iota(jnp.int32, (tokens, LANES), 1)

    def ids(n):
        return (lane + (first_column + n * LANES)).astype(F32)

    def allowed(col):
        return jnp.where(col >= V - CODES, 1.0, 0.0) == jnp.where(tgt[...] >= V - CODES, 1.0, 0.0)

    def peak_body(n, peak):
        cols = pl.ds(pl.multiple_of(n * LANES, LANES), LANES)
        value = jnp.where(allowed(ids(n)), logits[:, cols], NEG)
        logits[:, cols] = value
        return jnp.maximum(peak, value)

    peak = lax.fori_loop(0, columns // LANES, peak_body, jnp.full((tokens, LANES), NEG, F32))
    peak = jnp.max(peak, axis=1, keepdims=True)
    norm_b[...] = jnp.broadcast_to(peak, (tokens, LANES))

    def total_body(n, carry):
        total, hit = carry
        cols = pl.ds(pl.multiple_of(n * LANES, LANES), LANES)
        value = logits[:, cols]
        col = ids(n)
        total += jnp.where(allowed(col), jnp.exp(value - norm_b[...]), 0.0)
        hit += jnp.where(col == tgt[...], value, 0.0)
        return total, hit

    zero = jnp.zeros((tokens, LANES), F32)
    total, hit = lax.fori_loop(0, columns // LANES, total_body, (zero, zero))
    total = jnp.sum(total, axis=1, keepdims=True)
    hit = jnp.sum(hit, axis=1, keepdims=True)
    packed[...] = jnp.ones_like(packed)
    packed[0:tokens, :] = jnp.where(lane == 0, peak, jnp.where(lane == 1, total, hit))
    sb1[...] = packed[...].T[0:8]

    def combine(recv, n):
        top = recv[0, 0:1, :]
        for i in range(1, n):
            top = jnp.maximum(top, recv[i, 0:1, :])
        mass = jnp.zeros_like(top)
        value = jnp.zeros_like(top)
        for i in range(n):
            mass += recv[i, 1:2, :] * jnp.exp(recv[i, 0:1, :] - top)
            value += recv[i, 2:3, :]
        return top, mass, value

    rb1[mv] = sb1[...]
    copies = [send(sb1, rb1.at[mv], t1s.at[o], t1r.at[o], (me, v)) for o, v in enumerate(peers)]
    for copy in copies:
        copy.wait_recv()
    top, mass, value = combine(rb1, n_v)
    sb2[...] = jnp.zeros_like(sb2)
    sb2[0:1, :] = top
    sb2[1:2, :] = mass
    sb2[2:3, :] = value
    rb2[me] = sb2[...]
    copies = [send(sb2, rb2.at[me], t2s.at[o], t2r.at[o], (d, mv)) for o, d in enumerate(groups)]
    for copy in copies:
        copy.wait_recv()
    top, mass, value = combine(rb2, n_dp)
    log_norm = top + jnp.log(mass)
    token_lp = value - log_norm

    n_groups = cfg["groups"]
    pairs = n_groups // 2
    token = lax.broadcasted_iota(jnp.int32, token_lp.shape, 1)
    live, shifted, counts = [], [], []
    for i in range(n_groups):
        live.append((token >= i * WIN) & (token < i * WIN + lengths[i]))
        counts.append(jnp.full((1, 1), lengths[i], jnp.int32).astype(F32))
        policy = jnp.sum(jnp.where(live[i], token_lp, 0.0), axis=1, keepdims=True) / counts[i]
        shifted.append(policy - ref_logps[i])
    weights = [jnp.zeros((1, 1), F32) for _ in range(n_groups)]
    loss_sum = jnp.zeros((1, 1), F32)
    for k in range(pairs):
        signs = [
            jnp.where(pairing[2 * k] == i, 1.0, 0.0) - jnp.where(pairing[2 * k + 1] == i, 1.0, 0.0)
            for i in range(n_groups)
        ]
        margin = jnp.zeros((1, 1), F32)
        for i in range(n_groups):
            margin += signs[i] * shifted[i]
        margin = BETA * margin
        small = jnp.exp(-jnp.abs(margin))
        loss_sum += jnp.maximum(-margin, 0.0) + jnp.log1p(small)
        sigmoid = jnp.where(margin >= 0.0, small, 1.0) / (1.0 + small)
        pair_weight = -LOSS_SCALE * BETA * sigmoid / pairs
        for i in range(n_groups):
            weights[i] += signs[i] * pair_weight
    loss[0, 0] = (loss_sum / pairs)[0, 0]
    weight = jnp.zeros_like(token_lp)
    for i in range(n_groups):
        weight = jnp.where(live[i], weights[i] / counts[i], weight)
    spread[...] = jnp.zeros_like(spread)
    spread[0:1, :] = log_norm
    spread[1:2, :] = weight
    columns_of = spread[...].T
    norm_b[...] = jnp.broadcast_to(columns_of[0:tokens, 0:1], (tokens, LANES))
    weight_b[...] = jnp.broadcast_to(columns_of[0:tokens, 1:2], (tokens, LANES))

    def grad_body(n, carry):
        cols = pl.ds(pl.multiple_of(n * LANES, LANES), LANES)
        prob = jnp.exp(logits[:, cols] - norm_b[...])
        here = jnp.where(ids(n) == tgt[...], 1.0, 0.0)
        g[:, cols] = (weight_b[...] * (here - prob)).astype(BF16)
        return carry

    lax.fori_loop(0, columns // LANES, grad_body, 0)
    g_out = pltpu.make_async_copy(g, g_hbm, out_sem.at[2])
    g_out.start()

    span = half // RS_CHUNKS
    sub = min(512, span)

    def partial(row, store):
        def body(n, carry):
            at = pl.multiple_of(row + n * sub, sub)
            part = lax.dot_general(g[...], w[pl.ds(at, sub), :], (((1,), (1,)), ((), ())),
                                   preferred_element_type=F32)
            store(n * sub, part)
            return carry

        lax.fori_loop(0, span // sub, body, 0)

    pending = {}

    def scatter_stage(j, k):
        at = j * span
        lanes = slice(at, at + span)
        if k == 0:
            def keep_other(off, part):
                s1[:, pl.ds(pl.multiple_of(at + off, sub), sub)] = part.astype(BF16)

            partial((1 - core) * half + at, keep_other)
            ref = s1.at[:, pl.ds(at, span)]
            pending[j] = [send(ref, b1.at[:, pl.ds(at, span)], c1s.at[j], c1r.at[j], (me, mate))]

            def keep_own(off, part):
                acc[:, :, pl.ds(pl.multiple_of(at + off, sub), sub)] = part.reshape(n_dp, WIN, sub)

            partial(core * half + at, keep_own)
            return
        for copy in pending[j]:
            copy.wait_recv()
        if k == 1:
            acc[:, :, lanes] += b1[:, lanes].astype(F32).reshape(n_dp, WIN, span)
        else:
            q = bits - (k - 1)
            if q < bits and k <= bits + 1:
                _, held, _ = routes[q]
                for i, d in enumerate(held):
                    acc[d, :, lanes] += b2[(1 << q) - 1 + i, :, lanes].astype(F32)
        if k <= bits:
            q = bits - k
            partner, _, far = routes[q]
            copies = []
            for i, d in enumerate(far):
                slot = (1 << q) - 1 + i
                s2[slot, :, lanes] = acc[d, :, lanes].astype(BF16)
                sem = j * (n_dp - 1) + slot
                copies.append(send(s2.at[slot, :, pl.ds(at, span)], b2.at[slot, :, pl.ds(at, span)],
                                   c2s.at[sem], c2r.at[sem], (partner, mv)))
            pending[j] = copies
        elif k == bits + 1:
            mixed = lax.dot_general(perm, acc[me, :, lanes].astype(BF16), (((0,), (0,)), ((), ())),
                                    preferred_element_type=F32)
            s3[:, :, lanes] = mixed.reshape(n_v, 8, span).astype(BF16)
            b3[mv, :, lanes] = s3[mv, :, lanes]
            pending[j] = [
                send(s3.at[v, :, pl.ds(at, span)], b3.at[mv, :, pl.ds(at, span)],
                     c3s.at[j * n_v + o], c3r.at[j * n_v + o], (me, v))
                for o, v in enumerate(peers)
            ]
        else:
            for side in range(2):
                value = b3[side, :, lanes].astype(F32)
                for v in range(side + 2, n_v, 2):
                    value += b3[v, :, lanes].astype(F32)
                gh[:, side * half + at:side * half + at + span] = value[0:rows].astype(BF16)

    for t in range(RS_CHUNKS + bits + 2):
        for k in range(bits + 3):
            if 0 <= t - k < RS_CHUNKS:
                scatter_stage(t - k, k)

    for copy in sent:
        copy.wait_send()
    for copy in h_out:
        copy.wait()
    g_out.wait()


def head_kernel(h, g, out, turned):
    columns = g.shape[1]
    block = block_of(columns)
    turned[...] = h[...].astype(F32).T.astype(BF16)
    for n in range(columns // block):
        cols = slice(n * block, (n + 1) * block)
        out[:, cols] = jnp.dot(turned[...], g[:, cols], preferred_element_type=F32).astype(BF16)


def local(n_dp, n_v, hidden, head_weight, targets, image_mask, lengths, ref_logps, pairing):
    rows, depth = hidden.shape
    columns = head_weight.shape[1]
    tokens = rows * n_dp * n_v
    half = depth // 2
    wide = half + LANES
    tp = -(-tokens // LANES) * LANES
    dma = lambda n: pltpu.SemaphoreType.DMA((n,))
    smem = pl.BlockSpec(memory_space=pltpu.SMEM)
    vmem = pl.BlockSpec(memory_space=pltpu.VMEM)
    hbm = pl.BlockSpec(memory_space=pl.ANY)
    cfg = {"n_dp": n_dp, "n_v": n_v, "groups": lengths.shape[0]}
    grad_hidden, g, h, loss = pl.pallas_call(
        functools.partial(main_kernel, cfg),
        out_shape=(
            jax.ShapeDtypeStruct((rows, depth), BF16),
            jax.ShapeDtypeStruct((tokens, columns), BF16),
            jax.ShapeDtypeStruct((tokens, depth), BF16),
            jax.ShapeDtypeStruct((1, 1), F32),
        ),
        in_specs=[smem, smem, smem, smem, vmem, hbm],
        out_specs=(vmem, hbm, hbm, smem),
        scratch_shapes=[
            pltpu.VMEM((depth, columns), BF16),
            pltpu.VMEM((8, 2 * wide), BF16),
            pltpu.VMEM((tokens, 2 * wide), BF16),
            pltpu.VMEM((tokens, columns), F32),
            pltpu.VMEM((tokens, columns), BF16),
            pltpu.VMEM((n_v, 8, wide), BF16),
            pltpu.VMEM((tokens, LANES), F32),
            pltpu.VMEM((tokens, LANES), F32),
            pltpu.VMEM((tokens, LANES), F32),
            pltpu.VMEM((tp, LANES), F32),
            pltpu.VMEM((LANES, tp), F32),
            pltpu.VMEM((8, tp), F32),
            pltpu.VMEM((n_v, 8, tp), F32),
            pltpu.VMEM((8, tp), F32),
            pltpu.VMEM((n_dp, 8, tp), F32),
            pltpu.VMEM((tokens, half), BF16),
            pltpu.VMEM((tokens, half), BF16),
            pltpu.VMEM((n_dp, WIN, half), F32),
            pltpu.VMEM((n_dp - 1, WIN, half), BF16),
            pltpu.VMEM((n_dp - 1, WIN, half), BF16),
            pltpu.VMEM((n_v, 8, half), BF16),
            pltpu.VMEM((n_v, 8, half), BF16),
            dma(2 * AG_CHUNKS),
            dma(AG_CHUNKS * n_v), dma(AG_CHUNKS * n_v),
            dma(AG_CHUNKS * (n_dp - 1)), dma(AG_CHUNKS * (n_dp - 1)),
            dma(AG_CHUNKS), dma(AG_CHUNKS),
            dma(n_v), dma(n_v), dma(n_dp), dma(n_dp),
            dma(RS_CHUNKS), dma(RS_CHUNKS),
            dma(RS_CHUNKS * (n_dp - 1)), dma(RS_CHUNKS * (n_dp - 1)),
            dma(RS_CHUNKS * n_v), dma(RS_CHUNKS * n_v),
            dma(3),
        ],
        compiler_params=pltpu.CompilerParams(
            collective_id=0, has_side_effects=True, vmem_limit_bytes=67_000_000
        ),
        name="loss_and_hidden_gradient",
    )(targets, lengths, ref_logps, pairing, hidden, head_weight)
    tile = 512
    grad_head = pl.pallas_call(
        head_kernel,
        out_shape=jax.ShapeDtypeStruct((depth, columns), BF16),
        grid=(depth // tile,),
        in_specs=[pl.BlockSpec((tokens, tile), lambda i: (0, i)),
                  pl.BlockSpec((tokens, columns), lambda i: (0, 0))],
        out_specs=pl.BlockSpec((tile, columns), lambda i: (i, 0)),
        scratch_shapes=[pltpu.VMEM((tile, tokens), BF16)],
        compiler_params=pltpu.CompilerParams(vmem_limit_bytes=67_000_000),
        name="head_gradient",
    )(h, g)
    return grad_hidden, grad_head, loss.reshape(())


def solution(mesh):
    return jax.shard_map(
        functools.partial(local, mesh.shape["dp"], mesh.shape["vocab"]),
        mesh=mesh,
        in_specs=(
            P(("dp", "vocab"), None),
            P(None, ("dp", "vocab")),
            P(("dp", "vocab")),
            P(("dp", "vocab")),
            P(),
            P(),
            P(),
        ),
        out_specs=(P(("dp", "vocab"), None), P(None, ("dp", "vocab")), P()),
        check_vma=False,
    )
```

profile of v0, /device:TPU:0, one launch (start us, length us, event | category | flops | bytes accessed | tf_op | source)
XLA Modules:
  0.0 100.9 jit_solution(18265891737301032532)
XLA Ops:
  0.6 77.7 %loss_and_hidden_gradient.1 = (bf16[6,4096]{1,0:T(8,128)(2,1)}, bf16[192,5120]{1,0:T(8,128)(2,1)}, bf16[192,4096]{1,0:T(8,128)(2,1)}, f32[1,1]{1,0:T(1,128)}) custom-call(s32[6]{0:T(128)} %targets.1, s32[4]{0:T(128)} %lengths.1, f32[4]{0:T(128)} %ref_logps.1, s32[4]{0:T(128)} %pairing.1, bf16[6,4096]{1,0:T(8,128)(2,1)} %hidden.1, bf16[4096,5120]{1,0:T(8,128)(2,1)} %w_hbm.1), custom_call_target="tpu_custom_call" | custom-call | tf_op jit(solution)/shard_map/loss_and_hidden_gradient/pallas_call | solution.py:423
  78.3 19.3 %head_gradient.1 = bf16[4096,5120]{1,0:T(8,128)(2,1)} custom-call(bf16[192,4096]{1,0:T(8,128)(2,1)} %get-tuple-element.8.h, bf16[192,5120]{1,0:T(8,128)(2,1)} %get-tuple-element.9.g), custom_call_target="tpu_custom_call" | custom-call | tf_op jit(solution)/shard_map/head_gradient/pallas_call | solution.py:472
  97.6 1.5 %copy.11 = bf16[6,4096]{1,0:T(8,128)(2,1)} copy(bf16[6,4096]{1,0:T(8,128)(2,1)} %get-tuple-element.14) | data formatting | bytes 98304
where the time goes:
time: 101 us
  Pallas kernels  97 us (96%)
  between operations  2.39 us (2%)
  local copies, waits for them, and re-layouts  1.47 us (1%)
    pallas_call x1, Pallas kernels, local(): pl.pallas_call(functools.partial(main_kernel, cfg), out_shape=(jax.ShapeD...  77.7 us
    pallas_call x1, Pallas kernels, local(): pl.pallas_call(head_kernel, out_shape=jax.ShapeDtypeStruct((depth, column...  19.3 us

commit v1 on v0

v1 whole, which is shorter than its diff:
```python
import functools

import jax
import jax.numpy as jnp
from jax import lax
from jax.experimental import pallas as pl
from jax.experimental.pallas import tpu as pltpu
from jax.sharding import PartitionSpec as P

V = 163840
CODES = 32768
WIN = 48

NEG = -1e30
BETA = 1.0
LOSS_SCALE = 4096.0

AG_CHUNKS = 4
AHEAD = 2
RS_PARTS = (3, 3, 1, 1)
LANES = 128
MESH = pl.DeviceIdType.MESH
F32 = jnp.float32
BF16 = jnp.bfloat16


def block_of(size, top):
    block = top
    while size % block:
        block -= LANES
    return block


def main_kernel(cfg, targets, lengths, ref_logps, pairing, hidden, w_hbm, gh, g_hbm, h_hbm, loss,
                w, hid, h, logits, g, gt, r1, tgt, norm_b, weight_b, packed, spread, sb1, rb1, sb2, rb2,
                s1, b1, acc, s2, b2, s3, b3,
                w_sem, a1s, a1r, a2s, a2r, a3s, a3r, t1s, t1r, t2s, t2r,
                c1s, c1r, c2s, c2r, c3s, c3r, out_sem):
    n_dp, n_v = cfg["n_dp"], cfg["n_v"]
    tokens, columns = g.shape
    half = w.shape[0] // 2
    wide = half + LANES
    rows = tokens // (n_dp * n_v)
    me = lax.axis_index("dp")
    mv = lax.axis_index("vocab")
    core = lax.rem(mv, 2)
    mate = mv + 1 - 2 * core
    peers = [lax.rem(mv + o, n_v) for o in range(1, n_v)]
    groups = [lax.rem(me + o, n_dp) for o in range(1, n_dp)]

    step = half // AG_CHUNKS
    spans = [(j * step, step) for j in range(AG_CHUNKS)]

    loads = []
    for j, (at, size) in enumerate(spans):
        for side in range(2):
            span = pl.ds(side * half + at, size)
            loads.append(pltpu.make_async_copy(w_hbm.at[span, :], w.at[span, :], w_sem.at[2 * j + side]))
            loads[-1].start()

    spot = lax.broadcasted_iota(jnp.int32, (8, LANES), 0)
    digit = lax.broadcasted_iota(jnp.int32, (8, LANES), 1)
    tail = jnp.zeros((8, LANES), F32)
    for r in range(rows):
        number = targets[r]
        high, middle, low = number // 65536, lax.rem(number // 256, 256), lax.rem(number, 256)
        value = jnp.where(digit == 0, high, jnp.where(digit == 1, middle, low)).astype(F32)
        tail = jnp.where(spot == r, value, tail)
    hid[...] = jnp.zeros_like(hid)
    for side in range(2):
        hid[0:rows, side * wide:side * wide + half] = hidden[:, side * half:side * half + half]
        hid[:, side * wide + half:side * wide + wide] = tail.astype(BF16)

    barrier = pltpu.get_barrier_semaphore()
    for v in peers:
        pl.semaphore_signal(barrier, inc=1, device_id=(me, v), device_id_type=MESH)
    for d in groups:
        pl.semaphore_signal(barrier, inc=1, device_id=(d, mv), device_id_type=MESH)
    pl.semaphore_wait(barrier, n_v - 1 + n_dp - 1)

    sent = []

    def send(src, dst, s_sem, r_sem, device):
        copy = pltpu.make_async_remote_copy(
            src_ref=src, dst_ref=dst, send_sem=s_sem, recv_sem=r_sem, device_id=device, device_id_type=MESH)
        copy.start()
        sent.append(copy)
        return copy

    def window(index):
        return pl.ds(pl.multiple_of(index * WIN, 16), WIN)

    padded = n_v * 8
    r_id = lax.broadcasted_iota(jnp.int32, (WIN, padded), 0)
    s_id = lax.broadcasted_iota(jnp.int32, (WIN, padded), 1)
    perm = jnp.zeros((WIN, padded), F32)
    for v in range(n_v):
        perm = jnp.where((s_id - 8 * v == r_id - rows * v) & (s_id >= 8 * v) & (s_id < 8 * v + rows), 1.0, perm)
    perm = perm.astype(BF16)

    def wire(j):
        at, size = spans[j]
        return at, size + (LANES if j == AG_CHUNKS - 1 else 0)

    first = {}

    def spread_rows(j):
        at, size = wire(j)
        copies = []
        for o, v in enumerate(peers):
            col = pl.multiple_of(lax.rem(v, 2) * wide + at, LANES)
            copies.append(send(hid.at[:, pl.ds(col, size)], r1.at[mv, :, pl.ds(at, size)],
                               a1s.at[j * n_v + o], a1r.at[j * n_v + o], (me, v)))
        first[j] = copies

    for j in range(min(AHEAD, AG_CHUNKS)):
        spread_rows(j)

    waiting = {}

    def mine(j):
        at, size = wire(j)
        return pl.ds(pl.multiple_of(core * wide + at, LANES), size)

    def gather_stage(j, k):
        at, size = wire(j)
        if k == 0:
            r1[mv, :, at:at + size] = hid[:, mine(j)]
            for copy in first[j]:
                copy.wait_recv()
            if j + AHEAD < AG_CHUNKS:
                spread_rows(j + AHEAD)
            block = r1[:, :, at:at + size].astype(F32).reshape(padded, size).astype(BF16)
            h[window(me), mine(j)] = jnp.dot(perm, block, preferred_element_type=F32).astype(BF16)
        else:
            for copy in waiting[j]:
                copy.wait_recv()
        if k == 0:
            ref = h.at[window(me), mine(j)]
            waiting[j] = [
                send(ref, ref, a2s.at[j * (n_dp - 1) + o], a2r.at[j * (n_dp - 1) + o], (d, mv))
                for o, d in enumerate(groups)
            ]
        elif k == 1:
            ref = h.at[:, mine(j)]
            waiting[j] = [send(ref, ref, a3s.at[j], a3r.at[j], (me, mate))]
        else:
            multiply(j)

    block = block_of(columns, 2560)
    first_column = (me * n_v + mv) * columns
    lane = lax.broadcasted_iota(jnp.int32, (tokens, LANES), 1)

    def ids(n):
        return (lane + (first_column + n * LANES)).astype(F32)

    def multiply(j):
        at, size = spans[j]
        loads[2 * j].wait()
        loads[2 * j + 1].wait()
        last = j == AG_CHUNKS - 1
        if last:
            digits = h[:, half:half + LANES].astype(F32)
            target = digits[:, 0:1] * 65536.0 + digits[:, 1:2] * 256.0 + digits[:, 2:3]
            tgt[...] = jnp.broadcast_to(target, (tokens, LANES))
            norm_b[...] = jnp.full((tokens, LANES), NEG, F32)

        def body(n, carry):
            start = pl.multiple_of(n * block, block)
            cols = pl.ds(start, block)
            part = jnp.dot(jnp.concatenate([h[:, at:at + size], h[:, wide + at:wide + at + size]], axis=1),
                           jnp.concatenate([w[at:at + size, cols], w[half + at:half + at + size, cols]], axis=0),
                           preferred_element_type=F32)
            if j > 0:
                part = logits[:, cols] + part
            if not last:
                logits[:, cols] = part
                return carry
            coded = tgt[...] >= V - CODES
            peak = norm_b[...]
            for i in range(block // LANES):
                shared = (lane + (first_column + start + i * LANES) >= V - CODES) == coded
                value = jnp.where(shared, part[:, i * LANES:(i + 1) * LANES], NEG)
                logits[:, pl.ds(pl.multiple_of(start + i * LANES, LANES), LANES)] = value
                peak = jnp.maximum(peak, value)
            norm_b[...] = peak
            return carry

        lax.fori_loop(0, columns // block, body, 0)

    for t in range(AG_CHUNKS + 2):
        for k in range(3):
            if 0 <= t - k < AG_CHUNKS:
                gather_stage(t - k, k)

    h_out = [
        pltpu.make_async_copy(h.at[:, pl.ds(side * wide, half)], h_hbm.at[:, pl.ds(side * half, half)],
                              out_sem.at[side])
        for side in range(2)
    ]
    for copy in h_out:
        copy.start()

    peak = jnp.max(norm_b[...], axis=1, keepdims=True)
    norm_b[...] = jnp.broadcast_to(peak, (tokens, LANES))
    strips = columns // LANES
    unroll = 5 if strips % 5 == 0 else 1

    def total_body(m, carry):
        total, hit = carry
        for i in range(unroll):
            n = m * unroll + i
            value = logits[:, pl.ds(pl.multiple_of(n * LANES, LANES), LANES)]
            total += jnp.exp(value - norm_b[...])
            hit += jnp.where(ids(n) == tgt[...], value, 0.0)
        return total, hit

    zero = jnp.zeros((tokens, LANES), F32)
    total, hit = lax.fori_loop(0, strips // unroll, total_body, (zero, zero))
    total = jnp.sum(total, axis=1, keepdims=True)
    hit = jnp.sum(hit, axis=1, keepdims=True)
    packed[...] = jnp.ones_like(packed)
    packed[0:tokens, :] = jnp.where(lane == 0, peak, jnp.where(lane == 1, total, hit))
    turned = packed[...].T
    lines = packed.shape[0] // LANES

    def pack(dst, parts):
        dst[...] = jnp.zeros_like(dst)
        for b in range(lines):
            for q, part in enumerate(parts):
                dst[3 * b + q:3 * b + q + 1, :] = part[:, b * LANES:(b + 1) * LANES]

    def combine(recv, n):
        tops, masses, values = [], [], []
        for b in range(lines):
            top = recv[0, 3 * b:3 * b + 1, :]
            for i in range(1, n):
                top = jnp.maximum(top, recv[i, 3 * b:3 * b + 1, :])
            mass = jnp.zeros_like(top)
            value = jnp.zeros_like(top)
            for i in range(n):
                mass += recv[i, 3 * b + 1:3 * b + 2, :] * jnp.exp(recv[i, 3 * b:3 * b + 1, :] - top)
                value += recv[i, 3 * b + 2:3 * b + 3, :]
            tops.append(top)
            masses.append(mass)
            values.append(value)
        return [jnp.concatenate(x, axis=1) for x in (tops, masses, values)]

    pack(sb1, [turned[0:1], turned[1:2], turned[2:3]])
    rb1[mv] = sb1[...]
    copies = [send(sb1, rb1.at[mv], t1s.at[o], t1r.at[o], (me, v)) for o, v in enumerate(peers)]
    for copy in copies:
        copy.wait_recv()
    pack(sb2, combine(rb1, n_v))
    rb2[me] = sb2[...]
    copies = [send(sb2, rb2.at[me], t2s.at[o], t2r.at[o], (d, mv)) for o, d in enumerate(groups)]
    for copy in copies:
        copy.wait_recv()
    top, mass, value = combine(rb2, n_dp)
    log_norm = top + jnp.log(mass)
    token_lp = value - log_norm

    n_groups = cfg["groups"]
    pairs = n_groups // 2
    token = lax.broadcasted_iota(jnp.int32, token_lp.shape, 1)
    live, shifted, counts = [], [], []
    for i in range(n_groups):
        live.append((token >= i * WIN) & (token < i * WIN + lengths[i]))
        counts.append(jnp.full((1, 1), lengths[i], jnp.int32).astype(F32))
        policy = jnp.sum(jnp.where(live[i], token_lp, 0.0), axis=1, keepdims=True) / counts[i]
        shifted.append(policy - ref_logps[i])
    weights = [jnp.zeros((1, 1), F32) for _ in range(n_groups)]
    loss_sum = jnp.zeros((1, 1), F32)
    for k in range(pairs):
        signs = [
            jnp.where(pairing[2 * k] == i, 1.0, 0.0) - jnp.where(pairing[2 * k + 1] == i, 1.0, 0.0)
            for i in range(n_groups)
        ]
        margin = jnp.zeros((1, 1), F32)
        for i in range(n_groups):
            margin += signs[i] * shifted[i]
        margin = BETA * margin
        small = jnp.exp(-jnp.abs(margin))
        loss_sum += jnp.maximum(-margin, 0.0) + jnp.log1p(small)
        sigmoid = jnp.where(margin >= 0.0, small, 1.0) / (1.0 + small)
        pair_weight = -LOSS_SCALE * BETA * sigmoid / pairs
        for i in range(n_groups):
            weights[i] += signs[i] * pair_weight
    loss[0, 0] = (loss_sum / pairs)[0, 0]
    weight = jnp.zeros_like(token_lp)
    for i in range(n_groups):
        weight = jnp.where(live[i], weights[i] / counts[i], weight)
    spread[...] = jnp.zeros_like(spread)
    spread[0:1, :] = log_norm
    spread[1:2, :] = weight
    columns_of = spread[...].T
    norm_b[...] = jnp.broadcast_to(columns_of[0:tokens, 0:1], (tokens, LANES))
    weight_b[...] = jnp.broadcast_to(columns_of[0:tokens, 1:2], (tokens, LANES))

    wide_strip = block_of(columns, 512)

    def grad_body(m, carry):
        start = pl.multiple_of(m * wide_strip, wide_strip)
        for i in range(wide_strip // LANES):
            cols = pl.ds(pl.multiple_of(start + i * LANES, LANES), LANES)
            prob = jnp.exp(logits[:, cols] - norm_b[...])
            here = jnp.where((lane + (first_column + start + i * LANES)).astype(F32) == tgt[...], 1.0, 0.0)
            g[:, cols] = (weight_b[...] * (here - prob)).astype(BF16)
        gt[pl.ds(start, wide_strip), :] = g[:, pl.ds(start, wide_strip)].T
        return carry

    lax.fori_loop(0, columns // wide_strip, grad_body, 0)
    g_out = pltpu.make_async_copy(g, g_hbm, out_sem.at[2])
    g_out.start()

    chunks = []
    at = 0
    for part in RS_PARTS:
        chunks.append((at, half * part // sum(RS_PARTS)))
        at += chunks[-1][1]

    def partial(row, span):
        rows_of_w = pl.ds(pl.multiple_of(row, LANES), span)
        return jnp.dot(w[rows_of_w, :], gt[...], preferred_element_type=F32).T

    pending = {}

    def compute(j):
        at, span = chunks[j]
        lanes = slice(at, at + span)
        s1[:, lanes] = partial((1 - core) * half + at, span).astype(BF16)
        copy = send(s1.at[:, pl.ds(at, span)], b1.at[:, pl.ds(at, span)], c1s.at[j], c1r.at[j], (me, mate))
        acc[:, :, lanes] = partial(core * half + at, span).reshape(n_dp, WIN, span)
        copy.wait_recv()
        acc[:, :, lanes] += b1[:, lanes].astype(F32).reshape(n_dp, WIN, span)
        for o, d in enumerate(groups):
            s2[o, :, lanes] = acc[d, :, lanes].astype(BF16)
        pending[j] = [
            send(s2.at[o, :, pl.ds(at, span)], b2.at[o, :, pl.ds(at, span)],
                 c2s.at[j * (n_dp - 1) + o], c2r.at[j * (n_dp - 1) + o], (d, mv))
            for o, d in enumerate(groups)
        ]

    def across(j):
        at, span = chunks[j]
        lanes = slice(at, at + span)
        for copy in pending[j]:
            copy.wait_recv()
        value = acc[me, :, lanes]
        for o in range(n_dp - 1):
            value += b2[o, :, lanes].astype(F32)
        mixed = lax.dot_general(perm, value.astype(BF16), (((0,), (0,)), ((), ())), preferred_element_type=F32)
        s3[:, :, lanes] = mixed.reshape(n_v, 8, span).astype(BF16)
        b3[mv, :, lanes] = s3[mv, :, lanes]
        pending[j] = [
            send(s3.at[v, :, pl.ds(at, span)], b3.at[mv, :, pl.ds(at, span)],
                 c3s.at[j * n_v + o], c3r.at[j * n_v + o], (me, v))
            for o, v in enumerate(peers)
        ]

    def finish(j):
        at, span = chunks[j]
        lanes = slice(at, at + span)
        for copy in pending[j]:
            copy.wait_recv()
        for side in range(2):
            value = b3[side, :, lanes].astype(F32)
            for v in range(side + 2, n_v, 2):
                value += b3[v, :, lanes].astype(F32)
            gh[:, side * half + at:side * half + at + span] = value[0:rows].astype(BF16)

    n_chunks = len(chunks)
    for t in range(n_chunks + 2):
        if t < n_chunks:
            compute(t)
        if 0 <= t - 1 < n_chunks:
            across(t - 1)
        if 0 <= t - 2 < n_chunks:
            finish(t - 2)

    for copy in sent:
        copy.wait_send()
    for copy in h_out:
        copy.wait()
    g_out.wait()


def head_kernel(rc, nb, slots, gh_hbm, h_hbm, g_hbm, gh_out, out, h, g, turned, buf, load_sem, out_sem, gh_sem):
    depth, columns = out.shape
    n_rows, n_cols = depth // rc, columns // nb
    passed = pltpu.make_async_copy(gh_hbm, gh_out, gh_sem)
    h_in, g_in = [], []
    for r in range(2 * n_rows):
        span = pl.ds(r * rc // 2, rc // 2)
        h_in.append(pltpu.make_async_copy(h_hbm.at[:, span], h.at[:, span], load_sem.at[r]))
    for c in range(n_cols):
        span = pl.ds(c * nb, nb)
        g_in.append(pltpu.make_async_copy(g_hbm.at[:, span], g.at[:, span], load_sem.at[2 * n_rows + c]))
    h_in[0].start()
    g_in[0].start()
    for copy in h_in[1:] + g_in[1:]:
        copy.start()
    passed.start()
    busy = {}
    used = 0
    for c in range(n_cols):
        cols = slice(c * nb, (c + 1) * nb)
        for r in range(n_rows):
            span = slice(r * rc, (r + 1) * rc)
            if c == 0:
                for q in range(2 * r, 2 * r + 2):
                    h_in[q].wait()
                    piece = slice(q * rc // 2, (q + 1) * rc // 2)
                    turned[piece, :] = h[:, piece].T
            if r == 0:
                g_in[c].wait()
            slot = used % slots
            used += 1
            if slot in busy:
                busy[slot].wait()
            buf[slot] = jnp.dot(turned[span, :], g[:, cols], preferred_element_type=F32).astype(BF16)
            busy[slot] = pltpu.make_async_copy(buf.at[slot], out.at[pl.ds(r * rc, rc), pl.ds(c * nb, nb)],
                                               out_sem.at[slot])
            busy[slot].start()
    for copy in busy.values():
        copy.wait()
    passed.wait()


def local(n_dp, n_v, hidden, head_weight, targets, image_mask, lengths, ref_logps, pairing):
    rows, depth = hidden.shape
    columns = head_weight.shape[1]
    tokens = rows * n_dp * n_v
    half = depth // 2
    wide = half + LANES
    tp = -(-tokens // LANES) * LANES
    lines = -(-3 * (tp // LANES) // 8) * 8
    dma = lambda n: pltpu.SemaphoreType.DMA((n,))
    smem = pl.BlockSpec(memory_space=pltpu.SMEM)
    vmem = pl.BlockSpec(memory_space=pltpu.VMEM)
    hbm = pl.BlockSpec(memory_space=pl.ANY)
    cfg = {"n_dp": n_dp, "n_v": n_v, "groups": lengths.shape[0]}
    grad_hidden, g, h, loss = pl.pallas_call(
        functools.partial(main_kernel, cfg),
        out_shape=(
            jax.ShapeDtypeStruct((rows, depth), BF16),
            jax.ShapeDtypeStruct((tokens, columns), BF16),
            jax.ShapeDtypeStruct((tokens, depth), BF16),
            jax.ShapeDtypeStruct((1, 1), F32),
        ),
        in_specs=[smem, smem, smem, smem, vmem, hbm],
        out_specs=(vmem, hbm, hbm, smem),
        scratch_shapes=[
            pltpu.VMEM((depth, columns), BF16),
            pltpu.VMEM((8, 2 * wide), BF16),
            pltpu.VMEM((tokens, 2 * wide), BF16),
            pltpu.VMEM((tokens, columns), F32),
            pltpu.VMEM((tokens, columns), BF16),
            pltpu.VMEM((columns, tokens), BF16),
            pltpu.VMEM((n_v, 8, wide), BF16),
            pltpu.VMEM((tokens, LANES), F32),
            pltpu.VMEM((tokens, LANES), F32),
            pltpu.VMEM((tokens, LANES), F32),
            pltpu.VMEM((tp, LANES), F32),
            pltpu.VMEM((LANES, tp), F32),
            pltpu.VMEM((lines, LANES), F32),
            pltpu.VMEM((n_v, lines, LANES), F32),
            pltpu.VMEM((lines, LANES), F32),
            pltpu.VMEM((n_dp, lines, LANES), F32),
            pltpu.VMEM((tokens, half), BF16),
            pltpu.VMEM((tokens, half), BF16),
            pltpu.VMEM((n_dp, WIN, half), F32),
            pltpu.VMEM((n_dp - 1, WIN, half), BF16),
            pltpu.VMEM((n_dp - 1, WIN, half), BF16),
            pltpu.VMEM((n_v, 8, half), BF16),
            pltpu.VMEM((n_v, 8, half), BF16),
            dma(2 * AG_CHUNKS),
            dma(AG_CHUNKS * n_v), dma(AG_CHUNKS * n_v),
            dma(AG_CHUNKS * (n_dp - 1)), dma(AG_CHUNKS * (n_dp - 1)),
            dma(AG_CHUNKS), dma(AG_CHUNKS),
            dma(n_v), dma(n_v), dma(n_dp), dma(n_dp),
            dma(len(RS_PARTS)), dma(len(RS_PARTS)),
            dma(len(RS_PARTS) * (n_dp - 1)), dma(len(RS_PARTS) * (n_dp - 1)),
            dma(len(RS_PARTS) * n_v), dma(len(RS_PARTS) * n_v),
            dma(3),
        ],
        compiler_params=pltpu.CompilerParams(
            collective_id=0, has_side_effects=True, vmem_limit_bytes=67_000_000
        ),
        name="loss_and_hidden_gradient",
    )(targets, lengths, ref_logps, pairing, hidden, head_weight)
    rc, nb, slots = depth // 2, block_of(columns, 1024), 3
    grad_hidden, grad_head = pl.pallas_call(
        functools.partial(head_kernel, rc, nb, slots),
        out_shape=(jax.ShapeDtypeStruct((rows, depth), BF16), jax.ShapeDtypeStruct((depth, columns), BF16)),
        in_specs=[hbm, hbm, hbm],
        out_specs=(hbm, hbm),
        scratch_shapes=[
            pltpu.VMEM((tokens, depth), BF16),
            pltpu.VMEM((tokens, columns), BF16),
            pltpu.VMEM((depth, tokens), BF16),
            pltpu.VMEM((slots, rc, nb), BF16),
            dma(4 + columns // nb), dma(slots), pltpu.SemaphoreType.DMA,
        ],
        compiler_params=pltpu.CompilerParams(vmem_limit_bytes=67_000_000),
        name="head_gradient",
    )(grad_hidden, h, g)
    return grad_hidden, grad_head, loss.reshape(())


def solution(mesh):
    return jax.shard_map(
        functools.partial(local, mesh.shape["dp"], mesh.shape["vocab"]),
        mesh=mesh,
        in_specs=(
            P(("dp", "vocab"), None),
            P(None, ("dp", "vocab")),
            P(("dp", "vocab")),
            P(("dp", "vocab")),
            P(),
            P(),
            P(),
        ),
        out_specs=(P(("dp", "vocab"), None), P(None, ("dp", "vocab")), P()),
        check_vma=False,
    )
```

time: 101 us -> 97.2 us (0.962)
  Pallas kernels: 97 us -> 94.7 us
  local copies, waits for them, and re-layouts: 1.47 us -> 0 us
    pallas_call x1, Pallas kernels: 19.3 us -> 16.3 us  [local(): pl.pallas_call(functools.partial(head_kernel, rc, nb, slots), out_shape=(...]
    unnamed x1 -> x0, local copies, waits for them, and re-layouts: 1.47 us -> none
where the time goes in v1:
time: 97.2 us; the launch traced here: 97 us
  Pallas kernels  94.7 us (97%)
  between operations  2.34 us (2%)
    pallas_call x1, Pallas kernels, local(): pl.pallas_call(functools.partial(main_kernel, cfg), out_shape=(jax.ShapeD...  78.4 us
    pallas_call x1, Pallas kernels, local(): pl.pallas_call(functools.partial(head_kernel, rc, nb, slots), out_shape=(...  16.3 us

profile of v1, /device:TPU:0, one launch (start us, length us, event | category | flops | bytes accessed | tf_op | source)
XLA Modules:
  0.0 97.0 jit_solution(17327902786353197246)
XLA Ops:
  0.6 78.4 %loss_and_hidden_gradient.1 = (bf16[6,4096]{1,0:T(8,128)(2,1)}, bf16[192,5120]{1,0:T(8,128)(2,1)}, bf16[192,4096]{1,0:T(8,128)(2,1)}, f32[1,1]{1,0:T(1,128)}) custom-call(s32[6]{0:T(128)} %targets.1, s32[4]{0:T(128)} %lengths.1, f32[4]{0:T(128)} %ref_logps.1, s32[4]{0:T(128)} %pairing.1, bf16[6,4096]{1,0:T(8,128)(2,1)} %hidden.1, bf16[4096,5120]{1,0:T(8,128)(2,1)} %w_hbm.1), custom_call_target="tpu_custom_call" | custom-call | tf_op jit(solution)/shard_map/loss_and_hidden_gradient/pallas_call | solution.py:443
  79.0 16.3 %head_gradient.1 = (bf16[6,4096]{1,0:T(8,128)(2,1)}, bf16[4096,5120]{1,0:T(8,128)(2,1)}) custom-call(bf16[6,4096]{1,0:T(8,128)(2,1)} %get-tuple-element.9.gh_hbm, bf16[192,4096]{1,0:T(8,128)(2,1)} %get-tuple-element.10.h_hbm, bf16[192,5120]{1,0:T(8,128)(2,1)} %get-tuple-element.11.g_hbm), custom_call_target="tpu_custom_call" | custom-call | tf_op jit(solution)/shard_map/head_gradient/pallas_call | solution.py:493

commit v2 on v1

--- a/solution.py
+++ b/solution.py
@@ -188,10 +188,16 @@
 
         lax.fori_loop(0, columns // block, body, 0)
 
+    late = AG_CHUNKS - 1
     for t in range(AG_CHUNKS + 2):
-        for k in range(3):
-            if 0 <= t - k < AG_CHUNKS:
-                gather_stage(t - k, k)
+        if t < late:
+            gather_stage(t, 0)
+        if 0 <= t - 1 < AG_CHUNKS:
+            gather_stage(t - 1, 1)
+        if t == late - 1:
+            gather_stage(late, 0)
+        if 0 <= t - 2 < AG_CHUNKS:
+            gather_stage(t - 2, 2)
 
     h_out = [
         pltpu.make_async_copy(h.at[:, pl.ds(side * wide, half)], h_hbm.at[:, pl.ds(side * half, half)],
@@ -320,18 +326,29 @@
         at += chunks[-1][1]
 
     def partial(row, span):
-        rows_of_w = pl.ds(pl.multiple_of(row, LANES), span)
-        return jnp.dot(w[rows_of_w, :], gt[...], preferred_element_type=F32).T
+        size = span // 2
+        halves = []
+        for i in range(2):
+            rows_of_w = pl.ds(pl.multiple_of(row + i * size, LANES), size)
+            halves.append(jnp.dot(w[rows_of_w, :], gt[...], preferred_element_type=F32))
+        return jnp.concatenate([part.T for part in halves], axis=1)
 
     pending = {}
 
-    def compute(j):
+    def other(j):
+        at, span = chunks[j]
+        s1[:, at:at + span] = partial((1 - core) * half + at, span).astype(BF16)
+        pending[j] = [send(s1.at[:, pl.ds(at, span)], b1.at[:, pl.ds(at, span)], c1s.at[j], c1r.at[j], (me, mate))]
+
+    def own(j):
+        at, span = chunks[j]
+        acc[:, :, at:at + span] = partial(core * half + at, span).reshape(n_dp, WIN, span)
+
+    def join(j):
         at, span = chunks[j]
         lanes = slice(at, at + span)
-        s1[:, lanes] = partial((1 - core) * half + at, span).astype(BF16)
-        copy = send(s1.at[:, pl.ds(at, span)], b1.at[:, pl.ds(at, span)], c1s.at[j], c1r.at[j], (me, mate))
-        acc[:, :, lanes] = partial(core * half + at, span).reshape(n_dp, WIN, span)
-        copy.wait_recv()
+        for copy in pending[j]:
+            copy.wait_recv()
         acc[:, :, lanes] += b1[:, lanes].astype(F32).reshape(n_dp, WIN, span)
         for o, d in enumerate(groups):
             s2[o, :, lanes] = acc[d, :, lanes].astype(BF16)
@@ -370,9 +387,16 @@
             gh[:, side * half + at:side * half + at + span] = value[0:rows].astype(BF16)
 
     n_chunks = len(chunks)
+    other(0)
     for t in range(n_chunks + 2):
-        if t < n_chunks:
-            compute(t)
+        if t + 1 < n_chunks:
+            other(t + 1)
+        if t < n_chunks - 1:
+            own(t)
+            join(t)
+        if t == n_chunks - 2:
+            own(t + 1)
+            join(t + 1)
         if 0 <= t - 1 < n_chunks:
             across(t - 1)
         if 0 <= t - 2 < n_chunks:

time: 97.2 us -> 87.2 us (0.90)
  Pallas kernels: 94.7 us -> 84.6 us
    pallas_call x1, Pallas kernels: 78.4 us -> 68 us  [local(): pl.pallas_call(functools.partial(main_kernel, cfg), out_shape=(jax.ShapeD...]
where the time goes in v2:
time: 87.2 us; the launch traced here: 87 us
  Pallas kernels  84.6 us (97%)
  between operations  2.34 us (3%)
    pallas_call x1, Pallas kernels, local(): pl.pallas_call(functools.partial(main_kernel, cfg), out_shape=(jax.ShapeD...  68 us
    pallas_call x1, Pallas kernels, local(): pl.pallas_call(functools.partial(head_kernel, rc, nb, slots), out_shape=(...  16.6 us

profile of v2, /device:TPU:0, one launch (start us, length us, event | category | flops | bytes accessed | tf_op | source)
XLA Modules:
  0.0 87.0 jit_solution(6907614174410366761)
XLA Ops:
  0.6 68.0 %loss_and_hidden_gradient.1 = (bf16[6,4096]{1,0:T(8,128)(2,1)}, bf16[192,5120]{1,0:T(8,128)(2,1)}, bf16[192,4096]{1,0:T(8,128)(2,1)}, f32[1,1]{1,0:T(1,128)}) custom-call(s32[6]{0:T(128)} %targets.1, s32[4]{0:T(128)} %lengths.1, f32[4]{0:T(128)} %ref_logps.1, s32[4]{0:T(128)} %pairing.1, bf16[6,4096]{1,0:T(8,128)(2,1)} %hidden.1, bf16[4096,5120]{1,0:T(8,128)(2,1)} %w_hbm.1), custom_call_target="tpu_custom_call" | custom-call | tf_op jit(solution)/shard_map/loss_and_hidden_gradient/pallas_call | solution.py:467
  68.7 16.6 %head_gradient.1 = (bf16[6,4096]{1,0:T(8,128)(2,1)}, bf16[4096,5120]{1,0:T(8,128)(2,1)}) custom-call(bf16[6,4096]{1,0:T(8,128)(2,1)} %get-tuple-element.9.gh_hbm, bf16[192,4096]{1,0:T(8,128)(2,1)} %get-tuple-element.10.h_hbm, bf16[192,5120]{1,0:T(8,128)(2,1)} %get-tuple-element.11.g_hbm), custom_call_target="tpu_custom_call" | custom-call | tf_op jit(solution)/shard_map/head_gradient/pallas_call | solution.py:517
